TPU v7x, 32 devices: a whole 2x2x4 slice. The times are simulated.
32 devices in a mesh: batch: 4 (over y, x), seq: 8 (over z, core).
Axes of the slice: x: 2, y: 2, z: 4, core: 2. Of those that a mesh axis runs over, the one named last changes fastest.
Arguments:
- hidden: float32 [8192, 1024], P(('batch', 'seq')), may hold values from -6 to 6
- cotangent: float32 [8192, 1024], P(('batch', 'seq')), may hold values from -6 to 6
- norm_gain: bfloat16 [2, 1024], P(None, ('batch', 'seq')), may hold values from 0.099609375 to 1.8984375
- in_proj: bfloat16 [2, 1024, 4384], P(None, ('batch', 'seq')), may hold values from -0.1875 to 0.1875
- conv_weight: bfloat16 [2, 4, 2304], P(None, None, ('batch', 'seq')), may hold values from -3 to 3
- conv_bias: bfloat16 [2, 2304], P(None, ('batch', 'seq')), may hold values from -3 to 3
- dt_bias: float32 [2, 32], P(None, 'seq'), may hold values from -6 to -1
- a_log: float32 [2, 32], P(None, 'seq'), may hold values from -1.5 to 2.5
- d_skip: float32 [2, 32], P(None, 'seq'), may hold values from 0.5 to 1.5
- gate_gain: bfloat16 [2, 2048], P(None, ('batch', 'seq')), may hold values from 0.099609375 to 1.8984375
- out_proj: bfloat16 [2, 2048, 1024], P(None, ('batch', 'seq')), may hold values from -0.125 to 0.125
Outputs:
- output: float32 [8192, 1024], P(('batch', 'seq'))
- grad_hidden: float32 [8192, 1024], P(('batch', 'seq'))
- grad_norm_gain: float32 [2, 1024], P(None, ('batch', 'seq'))
- grad_in_proj: float32 [2, 1024, 4384], P(None, ('batch', 'seq'))
- grad_conv_weight: float32 [2, 4, 2304], P(None, None, ('batch', 'seq'))
- grad_conv_bias: float32 [2, 2304], P(None, ('batch', 'seq'))
- grad_dt_bias: float32 [2, 32], P(None, 'seq')
- grad_a_log: float32 [2, 32], P(None, 'seq')
- grad_d_skip: float32 [2, 32], P(None, 'seq')
- grad_gate_gain: float32 [2, 2048], P(None, ('batch', 'seq'))
- grad_out_proj: float32 [2, 2048, 1024], P(None, ('batch', 'seq'))
All inputs are finite; a program needn't handle non-finite values.
Results may differ from a plain program's by a relative error of at most 0.023.
Values may be sent and summed in bfloat16 or wider, within the bound.
No kernel may reach another device: no remote copies, remote signals or barrier semaphores. Data moves between devices by JAX's collectives and lax.ppermute only.
A program may use at most 320 MiB of HBM per device.

v0:
```python
import jax
import jax.numpy as jnp
from jax import lax
from jax.sharding import PartitionSpec as P

STATE = 128
SPAN = 256
SEQLEN = 2048
INNER = 2048
EPS = 1e-05
HIGHEST = lax.Precision.HIGHEST


def row_norm(rows, gain):
    factor = lax.rsqrt(jnp.mean(rows * rows, axis=-1, keepdims=True) + EPS)
    return rows * factor * gain


def causal_conv(signal, kernel, offset):
    taps = kernel.shape[0]
    length = signal.shape[0]
    padded = jnp.pad(signal, ((taps - 1, 0), (0, 0)))
    summed = offset + jnp.zeros_like(signal)
    for k in range(taps):
        summed = summed + kernel[k] * padded[k : k + length]
    return jax.nn.silu(summed)


def state_space(inputs, step_size, decay_rate, in_coef, out_coef):
    length, head_count, head_width = inputs.shape
    state_dim = in_coef.shape[1]
    blocks = length // SPAN
    blocked = inputs.reshape(blocks, SPAN, head_count, head_width)
    step_blk = step_size.reshape(blocks, SPAN, head_count)
    in_blk = in_coef.reshape(blocks, SPAN, state_dim)
    out_blk = out_coef.reshape(blocks, SPAN, state_dim)
    running = jnp.cumsum(step_blk * decay_rate, axis=1)
    run_heads = jnp.transpose(running, (0, 2, 1))
    step_heads = jnp.transpose(step_blk, (0, 2, 1))
    position = jnp.arange(SPAN)
    causal = (position[:, None] >= position[None, :])[None, None, :, :]
    spread = run_heads[:, :, :, None] - run_heads[:, :, None, :]
    decays = jnp.where(causal, jnp.exp(jnp.where(causal, spread, 0.0)), 0.0)
    scores = jnp.einsum("ctn,csn->cts", out_blk, in_blk, precision=HIGHEST)
    mixing = scores[:, None, :, :] * decays * step_heads[:, :, None, :]
    within = jnp.einsum("chts,cshp->cthp", mixing, blocked, precision=HIGHEST)
    to_end = jnp.exp(running[:, -1:, :] - running) * step_blk
    weighted = blocked * to_end[:, :, :, None]
    states = jnp.einsum("csn,cshp->chpn", in_blk, weighted, precision=HIGHEST)
    block_decay = jnp.exp(running[:, -1, :])

    def advance(carried, element):
        fresh, factor = element
        return (carried * factor[:, None, None] + fresh, carried)

    initial = jnp.zeros((head_count, head_width, state_dim), jnp.float32)
    _, entering = lax.scan(advance, initial, (states, block_decay))
    from_past = jnp.einsum("ctn,chpn->cthp", out_blk, entering, precision=HIGHEST)
    from_past = from_past * jnp.exp(running)[:, :, :, None]
    return (within + from_past).reshape(length, head_count, head_width)


def mixer(conv_x, conv_coef, gate_in, dt_raw, dt_shift, log_rate, skip_coef):
    length = conv_x.shape[0]
    head_count = dt_raw.shape[1]
    inputs = conv_x.reshape(length, head_count, -1)
    step_size = jax.nn.softplus(dt_raw + dt_shift)
    decay_rate = -jnp.exp(log_rate)
    half = conv_coef.shape[1] // 2
    mixed = state_space(inputs, step_size, decay_rate, conv_coef[:, :half], conv_coef[:, half:])
    mixed = mixed + skip_coef[None, :, None] * inputs
    return mixed.reshape(length, -1) * jax.nn.silu(gate_in)


def contract_rows(left, right):
    return lax.dot_general(
        left, right, (((0,), (0,)), ((), ())), preferred_element_type=jnp.float32
    )


def contract_cols(left, right):
    return lax.dot_general(
        left, right, (((1,), (1,)), ((), ())), preferred_element_type=jnp.float32
    )


def local(
    hidden,
    cotangent,
    norm_gain,
    in_proj,
    conv_weight,
    conv_bias,
    dt_bias,
    a_log,
    d_skip,
    gate_gain,
    out_proj,
):
    layers = in_proj.shape[0]
    pieces = lax.axis_size("seq")
    piece_index = lax.axis_index("seq")
    local_inner = INNER // pieces
    col_start = piece_index * local_inner
    conv_batch = jax.vmap(causal_conv, in_axes=(0, None, None))
    group_mix = jax.vmap(mixer, in_axes=(0, 0, 0, 0, None, None, None))
    stream = hidden
    stored = []
    for layer_idx in range(layers):
        gathered = (
            lax.all_gather(norm_gain[layer_idx], ("batch", "seq"), axis=0, tiled=True),
            lax.all_gather(in_proj[layer_idx], ("batch", "seq"), axis=0, tiled=True),
            lax.all_gather(conv_weight[layer_idx], ("batch", "seq"), axis=1, tiled=True),
            lax.all_gather(conv_bias[layer_idx], ("batch", "seq"), axis=0, tiled=True),
            lax.all_gather(gate_gain[layer_idx], ("batch", "seq"), axis=0, tiled=True),
            lax.all_gather(out_proj[layer_idx], ("batch", "seq"), axis=0, tiled=True),
        )
        n_gain, w_in, c_weight, c_bias, g_gain, w_out = gathered
        normed = row_norm(stream, n_gain.astype(jnp.float32)).astype(jnp.bfloat16)
        projected = jnp.dot(normed, w_in, preferred_element_type=jnp.float32).astype(jnp.bfloat16)
        gate_tok = projected[:, :INNER]
        x_tok = projected[:, INNER : 2 * INNER]
        coef_tok = projected[:, 2 * INNER : 2 * INNER + 2 * STATE]
        steps_tok = projected[:, 2 * INNER + 2 * STATE :]
        x_head, gate_head, steps_head = (
            lax.all_to_all(x_tok, "seq", split_axis=1, concat_axis=0, tiled=True),
            lax.all_to_all(gate_tok, "seq", split_axis=1, concat_axis=0, tiled=True),
            lax.all_to_all(steps_tok, "seq", split_axis=1, concat_axis=0, tiled=True),
        )
        coef_all = lax.all_gather(coef_tok, "seq", axis=0, tiled=True)
        group_rows = x_head.shape[0]
        seq_count = group_rows // SEQLEN
        kernel = jnp.concatenate(
            [lax.dynamic_slice_in_dim(c_weight, col_start, local_inner, 1), c_weight[:, INNER:]],
            axis=1,
        ).astype(jnp.float32)
        offset = jnp.concatenate(
            [lax.dynamic_slice_in_dim(c_bias, col_start, local_inner, 0), c_bias[INNER:]]
        ).astype(jnp.float32)
        signal = (
            jnp.concatenate([x_head, coef_all], axis=1)
            .astype(jnp.float32)
            .reshape(seq_count, SEQLEN, -1)
        )
        conv_out = conv_batch(signal, kernel, offset).astype(jnp.bfloat16)
        mix_args = (
            conv_out[:, :, :local_inner].astype(jnp.float32),
            conv_out[:, :, local_inner:].astype(jnp.float32),
            gate_head.astype(jnp.float32).reshape(seq_count, SEQLEN, -1),
            steps_head.astype(jnp.float32).reshape(seq_count, SEQLEN, -1),
            dt_bias[layer_idx],
            a_log[layer_idx],
            d_skip[layer_idx],
        )
        gated_head = group_mix(*mix_args).reshape(group_rows, -1).astype(jnp.bfloat16)
        gated = lax.all_to_all(gated_head, "seq", split_axis=0, concat_axis=1, tiled=True)
        gnormed = row_norm(gated.astype(jnp.float32), g_gain.astype(jnp.float32)).astype(
            jnp.bfloat16
        )
        stored.append((gathered, stream, normed, signal, kernel, offset, mix_args, gated, gnormed))
        stream = stream + jnp.dot(gnormed, w_out, preferred_element_type=jnp.float32)
    upstream = cotangent
    weight_parts = [None] * layers
    head_parts = [None] * layers
    for layer_idx in reversed(range(layers)):
        gathered, stream_in, normed, signal, kernel, offset, mix_args, gated, gnormed = stored[
            layer_idx
        ]
        gathered = (
            lax.all_gather(norm_gain[layer_idx], ("batch", "seq"), axis=0, tiled=True),
            lax.all_gather(in_proj[layer_idx], ("batch", "seq"), axis=0, tiled=True),
            lax.all_gather(conv_weight[layer_idx], ("batch", "seq"), axis=1, tiled=True),
            lax.all_gather(conv_bias[layer_idx], ("batch", "seq"), axis=0, tiled=True),
            lax.all_gather(gate_gain[layer_idx], ("batch", "seq"), axis=0, tiled=True),
            lax.all_gather(out_proj[layer_idx], ("batch", "seq"), axis=0, tiled=True),
        )
        n_gain, w_in, c_weight, c_bias, g_gain, w_out = gathered
        upstream_b = upstream.astype(jnp.bfloat16)
        grad_out = contract_rows(gnormed, upstream_b)
        d_gnormed = contract_cols(upstream_b, w_out)
        _, pull_gate = jax.vjp(row_norm, gated.astype(jnp.float32), g_gain.astype(jnp.float32))
        d_gated, grad_ggain = pull_gate(d_gnormed)
        d_head = lax.all_to_all(
            d_gated.astype(jnp.bfloat16), "seq", split_axis=1, concat_axis=0, tiled=True
        )
        group_rows = d_head.shape[0]
        seq_count = group_rows // SEQLEN
        _, pull_mix = jax.vjp(group_mix, *mix_args)
        d_convx, d_coef, d_gate, d_steps, grad_shift, grad_rate, grad_skip = pull_mix(
            d_head.astype(jnp.float32).reshape(seq_count, SEQLEN, -1)
        )
        _, pull_conv = jax.vjp(conv_batch, signal, kernel, offset)
        d_signal, grad_kernel, grad_offset = pull_conv(jnp.concatenate([d_convx, d_coef], axis=2))
        d_signal = d_signal.reshape(group_rows, -1)
        d_x_tok, d_gate_tok, d_steps_tok = (
            lax.all_to_all(
                d_signal[:, :local_inner].astype(jnp.bfloat16),
                "seq",
                split_axis=0,
                concat_axis=1,
                tiled=True,
            ),
            lax.all_to_all(
                d_gate.reshape(group_rows, -1).astype(jnp.bfloat16),
                "seq",
                split_axis=0,
                concat_axis=1,
                tiled=True,
            ),
            lax.all_to_all(
                d_steps.reshape(group_rows, -1).astype(jnp.bfloat16),
                "seq",
                split_axis=0,
                concat_axis=1,
                tiled=True,
            ),
        )
        d_coef_tok = lax.psum_scatter(
            d_signal[:, local_inner:].astype(jnp.bfloat16), "seq", scatter_dimension=0, tiled=True
        )
        d_projected = jnp.concatenate([d_gate_tok, d_x_tok, d_coef_tok, d_steps_tok], axis=1)
        grad_in = contract_rows(normed, d_projected)
        d_normed = contract_cols(d_projected, w_in)
        _, pull_norm = jax.vjp(row_norm, stream_in, n_gain.astype(jnp.float32))
        d_stream, grad_ngain = pull_norm(d_normed)
        upstream = upstream + d_stream
        zero_cols = jnp.zeros((grad_kernel.shape[0], INNER), jnp.float32)
        grad_conv_w = jnp.concatenate(
            [
                lax.dynamic_update_slice_in_dim(
                    zero_cols, grad_kernel[:, :local_inner], col_start, 1
                ),
                grad_kernel[:, local_inner:],
            ],
            axis=1,
        )
        zero_bias = jnp.zeros((INNER,), jnp.float32)
        grad_conv_b = jnp.concatenate(
            [
                lax.dynamic_update_slice_in_dim(zero_bias, grad_offset[:local_inner], col_start, 0),
                grad_offset[local_inner:],
            ]
        )
        head_parts[layer_idx] = lax.psum((grad_shift, grad_rate, grad_skip), "batch")
        weight_parts[layer_idx] = (
            grad_ngain,
            grad_in,
            grad_conv_w,
            grad_conv_b,
            grad_ggain,
            grad_out,
        )
    stacked = tuple((jnp.stack([weight_parts[i][k] for i in range(layers)]) for k in range(6)))
    partial_sums = (
        lax.psum_scatter(
            stacked[0].astype(jnp.bfloat16), "batch", scatter_dimension=1, tiled=True
        ).astype(jnp.float32),
        lax.psum_scatter(
            stacked[1].astype(jnp.bfloat16), "batch", scatter_dimension=1, tiled=True
        ).astype(jnp.float32),
        lax.psum_scatter(
            stacked[2].astype(jnp.bfloat16), "batch", scatter_dimension=2, tiled=True
        ).astype(jnp.float32),
        lax.psum_scatter(
            stacked[3].astype(jnp.bfloat16), "batch", scatter_dimension=1, tiled=True
        ).astype(jnp.float32),
        lax.psum_scatter(
            stacked[4].astype(jnp.bfloat16), "batch", scatter_dimension=1, tiled=True
        ).astype(jnp.float32),
        lax.psum_scatter(
            stacked[5].astype(jnp.bfloat16), "batch", scatter_dimension=1, tiled=True
        ).astype(jnp.float32),
    )
    stacked = (
        lax.psum_scatter(
            partial_sums[0].astype(jnp.bfloat16), "seq", scatter_dimension=1, tiled=True
        ).astype(jnp.float32),
        lax.psum_scatter(
            partial_sums[1].astype(jnp.bfloat16), "seq", scatter_dimension=1, tiled=True
        ).astype(jnp.float32),
        lax.psum_scatter(
            partial_sums[2].astype(jnp.bfloat16), "seq", scatter_dimension=2, tiled=True
        ).astype(jnp.float32),
        lax.psum_scatter(
            partial_sums[3].astype(jnp.bfloat16), "seq", scatter_dimension=1, tiled=True
        ).astype(jnp.float32),
        lax.psum_scatter(
            partial_sums[4].astype(jnp.bfloat16), "seq", scatter_dimension=1, tiled=True
        ).astype(jnp.float32),
        lax.psum_scatter(
            partial_sums[5].astype(jnp.bfloat16), "seq", scatter_dimension=1, tiled=True
        ).astype(jnp.float32),
    )
    heads_stacked = tuple((jnp.stack([head_parts[i][k] for i in range(layers)]) for k in range(3)))
    return (
        stream,
        upstream,
        stacked[0],
        stacked[1],
        stacked[2],
        stacked[3],
        heads_stacked[0],
        heads_stacked[1],
        heads_stacked[2],
        stacked[4],
        stacked[5],
    )


def solution(mesh):
    in_specs = (
        P(("batch", "seq"), None),
        P(("batch", "seq"), None),
        P(None, ("batch", "seq")),
        P(None, ("batch", "seq"), None),
        P(None, None, ("batch", "seq")),
        P(None, ("batch", "seq")),
        P(None, "seq"),
        P(None, "seq"),
        P(None, "seq"),
        P(None, ("batch", "seq")),
        P(None, ("batch", "seq"), None),
    )
    out_specs = (
        P(("batch", "seq"), None),
        P(("batch", "seq"), None),
        P(None, ("batch", "seq")),
        P(None, ("batch", "seq"), None),
        P(None, None, ("batch", "seq")),
        P(None, ("batch", "seq")),
        P(None, "seq"),
        P(None, "seq"),
        P(None, "seq"),
        P(None, ("batch", "seq")),
        P(None, ("batch", "seq"), None),
    )
    return jax.shard_map(local, mesh=mesh, in_specs=in_specs, out_specs=out_specs, check_vma=False)
```

profile of v0, /device:TPU:0, one launch (start us, length us, event | category | flops | bytes accessed | tf_op | source)
XLA Modules:
  0.0 1634.4 jit_solution(17287218793255971408)
XLA Ops:
  12.8 43.6 %all-reduce.36 = (bf16[1024]{0:T(1024)(128)(2,1)S(1)}, bf16[2304]{0:T(1024)(128)(2,1)S(1)}, bf16[2048]{0:T(1024)(128)(2,1)}, bf16[1024]{0:T(1024)(128)(2,1)}, bf...) all-reduce(bf16[1024]{0:T(1024)(128)(2,1)S(1)} %dynamic-update-slic, ...), channel_id=4, replica_groups=mesh['batch'=4,'seq'=8] {'batch','seq'}, use_global_device_ids=true, to_apply=%add.27 | all-reduce | flops 10752 | bytes 43008
  57.1 37.6 %all-gather.23.cloned.1.call-done = bf16[1,1024,4384]{2,1,0:T(8,128)(2,1)} async-done(((bf16[1,32,4384]{2,1,0:T(8,128)(2,1)}), bf16[1,1024,4384]{2,1,0:T(8,128)(2,1)}) %all-gather.23.cloned.1.call-update) | async-done | bytes 8978448 | tf_op jit(solution)/shard_map/all_gather | solution.py:112
  105.8 47.1 %all-gather.1 = bf16[1,4,2304]{1,0,2:T(2,128)(2,1)S(1)} all-gather(bf16[1,4,72]{1,0,2:T(2,128)(2,1)S(1)} %copy.1540), channel_id=3, replica_groups=mesh['batch'=4,'seq'=8] {'batch','seq'}, dimensions={2}, use_global_device_ids=true | all-gather | bytes 19008 | tf_op jit(solution)/shard_map/all_gather | solution.py:113
  154.3 48.1 %all-gather.7 = bf16[1,4,2304]{1,0,2:T(2,128)(2,1)S(1)} all-gather(bf16[1,4,72]{1,0,2:T(2,128)(2,1)S(1)} %copy.1539), channel_id=9, replica_groups=mesh['batch'=4,'seq'=8] {'batch','seq'}, dimensions={2}, use_global_device_ids=true | all-gather | bytes 19008 | tf_op jit(solution)/shard_map/all_gather | solution.py:113
  230.5 28.3 %all-to-all-done = bf16[256,8,256]{0,2,1:T(8,128)(2,1)S(1)} async-done(((bf16[256,8,256]{0,2,1:T(8,128)(2,1)}), bf16[256,8,256]{0,2,1:T(8,128)(2,1)S(1)}, u32[]{:S(2)}, u32[]{:S(2)}) %all-to-all-start) | async-done | bytes 1048608 | tf_op jit(solution)/shard_map/all_to_all | solution.py:126
  326.1 26.4 %all-to-all-done.3 = bf16[8,256,256]{1,2,0:T(8,128)(2,1)S(1)} async-done(((bf16[8,256,256]{1,2,0:T(8,128)(2,1)}), bf16[8,256,256]{1,2,0:T(8,128)(2,1)S(1)}, u32[]{:S(2)}, u32[]{:S(2)}) %all-to-all-start.3) | async-done | bytes 1048608 | tf_op jit(solution)/shard_map/all_to_all | solution.py:156
  400.9 15.1 all-to-all-done.4
  441.2 18.9 %while.95 = (s32[]{:T(128)}, f32[1,4,64,128]{3,2,1,0:T(8,128)S(1)}, f32[8,1,4,64,128]{4,3,2,1,0:T(8,128)}, f32[8,1,4]{2,1,0:T(1,128)}, f32[8,1,4,64,128]{4,3,2,1,0:T(8,128)}, /*index=5*/s32[]{:T(128)}, s32[]{:T(128)}) while((s32[]{:T(128)}, f32[1,4,64,128]{3,2,1,0:T(8,128)S(1)}, f32[8,1,4,64,128]{4,3,2,1,0:T(8,128)}, ...), condition=%wide.region_10.11_spmd.clone, body=%wide.region_9.10_spmd.clone.sunk | while | flops 131075 | bytes 655516 | solution.py:57
  514.7 11.3 all-to-all-done.7
  545.3 18.3 %while.96 = (s32[]{:T(128)}, f32[1,4,64,128]{3,2,1,0:T(8,128)S(1)}, f32[8,1,4,64,128]{4,3,2,1,0:T(8,128)S(1)}, f32[8,1,4,1,1]{2,4,3,1,0:T(1,128)S(1)}, f32[8,1,4...) while((s32[]{:T(128)}, f32[1,4,64,128]{3,2,1,0:T(8,128)S(1)}, ...), condition=%wide.region_15.17_spmd.clone, body=%wide.region_14.16_spmd.clone.sunk | while | flops 131075 | bytes 656056 | solution.py:57
  579.6 13.8 fusion.53
  599.8 14.4 while.97
  624.9 10.3 reduce-window.50
  682.4 10.4 bitcast_add_fusion.8
  730.8 31.5 %all-to-all-done.10 = bf16[8,256,256]{1,2,0:T(8,128)(2,1)S(1)} async-done(((bf16[8,256,256]{1,2,0:T(8,128)(2,1)}), bf16[8,256,256]{1,2,0:T(8,128)(2,1)S(1)}, u32[]{:S(2)}, u32[]{:S(2)}) %all-to-all-start.10) | async-done | bytes 1048608 | tf_op jit(solution)/shard_map/all_to_all | solution.py:196
  815.3 32.0 %while.98 = (s32[]{:T(128)}, f32[1,4,64,128]{3,2,1,0:T(8,128)S(1)}, f32[8,1,4,64,128]{4,3,2,1,0:T(8,128)}, f32[8,1,4,1,1]{2,4,3,1,0:T(1,128)}, f32[8,1,4]{2,1,0:...) while((s32[]{:T(128)}, f32[1,4,64,128]{3,2,1,0:T(8,128)S(1)}, ...), condition=%wide.region_34.36_spmd.clone, body=%wide.region_33.35_spmd.clone.sunk | while | flops 131075 | bytes 918696 | solution.py:57
  855.0 13.4 fusion.55
  875.3 19.3 %while.99 = (s32[]{:T(128)}, f32[1,4,64,128]{3,2,1,0:T(8,128)S(1)}, f32[8,1,4,64,128]{4,3,2,1,0:T(8,128)}, f32[8,1,4]{2,1,0:T(1,128)S(1)}, f32[8,1,4,64,128]{4,3...) while((s32[]{:T(128)}, f32[1,4,64,128]{3,2,1,0:T(8,128)S(1)}, ...), condition=%wide.region_38.40_spmd.clone, body=%wide.region_36.39_spmd.clone.sunk | while | flops 196608 | bytes 1049812 | solution.py:57
  905.3 10.1 reduce-window.56
  963.2 10.6 bitcast_add_fusion.6
  1011.9 31.9 %all-to-all-done.14 = bf16[8,256,256]{1,2,0:T(8,128)(2,1)} async-done(((bf16[8,256,256]{1,2,0:T(8,128)(2,1)}), bf16[8,256,256]{1,2,0:T(8,128)(2,1)}, u32[]{:S(2)}, u32[]{:S(2)}) %all-to-all-start.14) | async-done | bytes 1048608 | tf_op jit(solution)/shard_map/all_to_all | solution.py:196
  1059.1 15.5 all-to-all-done.13
  1104.7 11.5 pad_maximum_fusion
  1125.2 71.6 %reduce-scatter.32.cloned.1.call-done = bf16[2,512,1024]{2,1,0:T(8,128)(2,1)} async-done(((bf16[2,2048,1024]{2,1,0:T(8,128)(2,1)}), bf16[2,512,1024]{2,1,0:T(8,128)(2,1)}) %reduce-scatter.32.cloned.1.call-update) | async-done | bytes 2097168 | tf_op jit(solution)/shard_map/reduce_scatter | solution.py:270
  1196.9 166.3 %reduce-scatter.30.cloned.1.call-done = bf16[2,256,4384]{1,2,0:T(8,128)(2,1)} async-done(((bf16[2,1024,4384]{1,2,0:T(8,128)(2,1)}), bf16[2,256,4384]{1,2,0:T(8,128)(2,1)}) %reduce-scatter.30.cloned.1.call-update) | async-done | bytes 4489232 | tf_op jit(solution)/shard_map/reduce_scatter | solution.py:258
  1363.2 12.5 copy.1465
  1383.2 12.8 reduce-scatter.46.cloned.1.call-done
  1409.2 13.1 reduce-scatter.42.cloned.1.call-done
  1423.3 27.7 %reduce-scatter.40.cloned.1.call-done = bf16[576,8]{1,0:T(8,128)(2,1)} async-done(((bf16[2304,8]{1,0:T(8,128)(2,1)}), bf16[576,8]{1,0:T(8,128)(2,1)}) %reduce-scatter.40.cloned.1.call-update) | async-done | bytes 9232
  1452.3 28.2 %all-reduce.37 = (bf16[2,4,576]{2,1,0:T(4,128)(2,1)S(1)}, bf16[2,576]{1,0:T(2,128)(2,1)S(1)}) all-reduce(bf16[2,4,576]{2,1,0:T(4,128)(2,1)S(1)} %copy.1526, bf16[2,576]{1,0:T(2,128)(2,1)S(1)} %copy.1530), channel_id=21, replica_groups=mesh['batch'=4,'seq'=8] {'seq'}, use_global_device_ids=true, to_apply=%region_65.67.clone | all-reduce | flops 5760 | bytes 23040
  1486.0 33.8 %reduce-scatter.34.cloned.1.call-done = bf16[2,64,1024]{2,1,0:T(8,128)(2,1)} async-done(((bf16[2,512,1024]{2,1,0:T(8,128)(2,1)}), bf16[2,64,1024]{2,1,0:T(8,128)(2,1)}) %reduce-scatter.34.cloned.1.call-update) | async-done | bytes 262160 | tf_op jit(solution)/shard_map/reduce_scatter | solution.py:290
  1521.5 103.2 %all-reduce.40.cloned.1.call-done = bf16[2,256,4384]{2,0,1:T(2,128)(2,1)} async-done(((bf16[2,256,4384]{2,0,1:T(2,128)(2,1)}), bf16[2,256,4384]{2,0,1:T(2,128)(2,1)}) %all-reduce.40.cloned.1.call-update) | async-done | bytes 4489232
  (1037 shorter events, 735.2 us)
Async XLA Ops:
  7.2 87.5 %all-gather.23.cloned.1.call-start = ((), (), s32[]{:S(2)}) async-start(), calls=%async_computation.34 | async-start | bytes 9461760 | tf_op jit(solution)/shard_map/all_gather | solution.py:112
  9.2 255.2 %all-gather.19.cloned.1.call-start = ((), (), s32[]{:S(2)}) async-start(), calls=%async_computation.27 | async-start | bytes 1179648 | tf_op jit(solution)/shard_map/all_gather | solution.py:130
  104.2 252.1 %all-gather.25.cloned.1.call-start = ((), (), s32[]{:S(2)}) async-start(), calls=%async_computation.35 | async-start | bytes 4325376 | tf_op jit(solution)/shard_map/all_gather | solution.py:116
  105.0 255.7 %all-gather.27.cloned.1.call-start = ((), (), s32[]{:S(2)}) async-start(), calls=%async_computation.36 | async-start | bytes 9461760 | tf_op jit(solution)/shard_map/all_gather | solution.py:112
  216.5 42.3 %all-to-all-start = ((bf16[256,8,256]{0,2,1:T(8,128)(2,1)}), bf16[256,8,256]{0,2,1:T(8,128)(2,1)S(1)}, u32[]{:S(2)}, u32[]{:S(2)}) async-start(bf16[256,8,256]{0,2,1:T(8,128)(2,1)} %bitcast.6), calls=%async_computation | async-start | bytes 2097152 | tf_op jit(solution)/shard_map/all_to_all | solution.py:126
  258.8 51.6 %all-to-all-start.2 = ((bf16[256,8,256]{0,2,1:T(8,128)(2,1)}), bf16[256,8,256]{0,2,1:T(8,128)(2,1)}, u32[]{:S(2)}, u32[]{:S(2)}) async-start(bf16[256,8,256]{0,2,1:T(8,128)(2,1)} %bitcast.39), calls=%async_computation.2 | async-start | bytes 2097152 | tf_op jit(solution)/shard_map/all_to_all | solution.py:127
  322.4 30.1 %all-to-all-start.3 = ((bf16[8,256,256]{1,2,0:T(8,128)(2,1)}), bf16[8,256,256]{1,2,0:T(8,128)(2,1)S(1)}, u32[]{:S(2)}, u32[]{:S(2)}) async-start(bf16[8,256,256]{1,2,0:T(8,128)(2,1)} %copy.1331), calls=%async_computation.3 | async-start | bytes 2097152 | tf_op jit(solution)/shard_map/all_to_all | solution.py:156
  326.0 97.5 %all-gather.21.cloned.1.call-start = ((), (), s32[]{:S(2)}) async-start(), calls=%async_computation.28 | async-start | bytes 1179648 | tf_op jit(solution)/shard_map/all_gather | solution.py:130
  370.5 162.5 %all-gather.29.cloned.1.call-start = ((), (), s32[]{:S(2)}) async-start(), calls=%async_computation.37 | async-start | bytes 4325376 | tf_op jit(solution)/shard_map/all_gather | solution.py:116
  383.8 32.3 %all-to-all-start.4 = ((bf16[256,8,256]{0,2,1:T(8,128)(2,1)}), bf16[256,8,256]{0,2,1:T(8,128)(2,1)S(1)}, u32[]{:S(2)}, u32[]{:S(2)}) async-start(bf16[256,8,256]{0,2,1:T(8,128)(2,1)} %bitcast.996), calls=%async_computation.4 | async-start | bytes 2097152 | tf_op jit(solution)/shard_map/all_to_all | solution.py:126
  416.1 65.3 %all-to-all-start.6 = ((bf16[256,8,256]{0,2,1:T(8,128)(2,1)}), bf16[256,8,256]{0,2,1:T(8,128)(2,1)}, u32[]{:S(2)}, u32[]{:S(2)}) async-start(bf16[256,8,256]{0,2,1:T(8,128)(2,1)} %bitcast.995), calls=%async_computation.6 | async-start | bytes 2097152 | tf_op jit(solution)/shard_map/all_to_all | solution.py:127
  494.3 31.7 %all-to-all-start.7 = ((bf16[8,256,256]{1,2,0:T(8,128)(2,1)}), bf16[8,256,256]{1,2,0:T(8,128)(2,1)}, u32[]{:S(2)}, u32[]{:S(2)}) async-start(bf16[8,256,256]{1,2,0:T(8,128)(2,1)} %copy.1359), calls=%async_computation.7 | async-start | bytes 2097152 | tf_op jit(solution)/shard_map/all_to_all | solution.py:156
  541.5 30.2 %all-to-all-start.8 = ((bf16[256,8,256]{0,2,1:T(8,128)(2,1)}), bf16[256,8,256]{0,2,1:T(8,128)(2,1)S(1)}, u32[]{:S(2)}, u32[]{:S(2)}) async-start(bf16[256,8,256]{0,2,1:T(8,128)(2,1)} %bitcast.115), calls=%async_computation.8 | async-start | bytes 2097152 | tf_op jit(solution)/shard_map/all_to_all | solution.py:183
  649.6 73.9 %all-to-all-start.11 = ((bf16[8,256,4]{1,2,0:T(4,128)(2,1)}), bf16[8,256,4]{1,2,0:T(4,128)(2,1)S(1)}, u32[]{:S(2)}, u32[]{:S(2)}) async-start(bf16[8,256,4]{1,2,0:T(4,128)(2,1)} %bitcast.163), calls=%async_computation.12 | async-start | bytes 32768 | tf_op jit(solution)/shard_map/all_to_all | solution.py:210
  723.5 38.8 %all-to-all-start.10 = ((bf16[8,256,256]{1,2,0:T(8,128)(2,1)}), bf16[8,256,256]{1,2,0:T(8,128)(2,1)S(1)}, u32[]{:S(2)}, u32[]{:S(2)}) async-start(bf16[8,256,256]{1,2,0:T(8,128)(2,1)} %bitcast.912), calls=%async_computation.10 | async-start | bytes 2097152 | tf_op jit(solution)/shard_map/all_to_all | solution.py:196
  728.5 64.6 %reduce-scatter.26.cloned.1.call-start = ((), (), s32[]{:S(2)}) async-start(), calls=%async_computation.29 | async-start | bytes 1179648 | tf_op jit(solution)/shard_map/reduce_scatter | solution.py:218
  762.3 30.8 %all-to-all-start.9 = ((bf16[8,256,256]{1,2,0:T(8,128)(2,1)}), bf16[8,256,256]{1,2,0:T(8,128)(2,1)}, u32[]{:S(2)}, u32[]{:S(2)}) async-start(bf16[8,256,256]{1,2,0:T(8,128)(2,1)} %copy.1384), calls=%async_computation.9 | async-start | bytes 2097152 | tf_op jit(solution)/shard_map/all_to_all | solution.py:203
  808.8 38.4 %all-to-all-start.12 = ((bf16[256,8,256]{0,2,1:T(8,128)(2,1)}), bf16[256,8,256]{0,2,1:T(8,128)(2,1)}, u32[]{:S(2)}, u32[]{:S(2)}) async-start(bf16[256,8,256]{0,2,1:T(8,128)(2,1)} %bitcast.990), calls=%async_computation.13 | async-start | bytes 2097152 | tf_op jit(solution)/shard_map/all_to_all | solution.py:183
  928.7 75.6 %all-to-all-start.15 = ((bf16[8,256,4]{1,2,0:T(4,128)(2,1)}), bf16[8,256,4]{1,2,0:T(4,128)(2,1)S(1)}, u32[]{:S(2)}, u32[]{:S(2)}) async-start(bf16[8,256,4]{1,2,0:T(4,128)(2,1)} %bitcast.238), calls=%async_computation.17 | async-start | bytes 32768 | tf_op jit(solution)/shard_map/all_to_all | solution.py:210
  1004.3 39.5 %all-to-all-start.14 = ((bf16[8,256,256]{1,2,0:T(8,128)(2,1)}), bf16[8,256,256]{1,2,0:T(8,128)(2,1)}, u32[]{:S(2)}, u32[]{:S(2)}) async-start(bf16[8,256,256]{1,2,0:T(8,128)(2,1)} %bitcast.911), calls=%async_computation.15 | async-start | bytes 2097152 | tf_op jit(solution)/shard_map/all_to_all | solution.py:196
  1009.6 65.0 %reduce-scatter.28.cloned.1.call-start = ((), (), s32[]{:S(2)}) async-start(), calls=%async_computation.30 | async-start | bytes 1179648 | tf_op jit(solution)/shard_map/reduce_scatter | solution.py:218
  1043.8 30.8 %all-to-all-start.13 = ((bf16[8,256,256]{1,2,0:T(8,128)(2,1)}), bf16[8,256,256]{1,2,0:T(8,128)(2,1)}, u32[]{:S(2)}, u32[]{:S(2)}) async-start(bf16[8,256,256]{1,2,0:T(8,128)(2,1)} %copy.1436), calls=%async_computation.14 | async-start | bytes 2097152 | tf_op jit(solution)/shard_map/all_to_all | solution.py:203
  1048.0 69.2 %reduce-scatter.44.cloned.1.call-start = ((), (), s32[]{:S(2)}) async-start(), calls=%async_computation.42 | async-start | bytes 655360
  1054.1 70.6 %reduce-scatter.36.cloned.1.call-start = ((), (), s32[]{:S(2)}) async-start(), calls=%async_computation.38 | async-start | bytes 327680
  1083.8 113.0 %reduce-scatter.32.cloned.1.call-start = ((), (), s32[]{:S(2)}) async-start(), calls=%async_computation.32 | async-start | bytes 10485760 | tf_op jit(solution)/shard_map/reduce_scatter | solution.py:270
  1091.4 271.7 %reduce-scatter.30.cloned.1.call-start = ((), (), s32[]{:S(2)}) async-start(), calls=%async_computation.31 | async-start | bytes 22446080 | tf_op jit(solution)/shard_map/reduce_scatter | solution.py:258
  1116.2 279.8 %reduce-scatter.46.cloned.1.call-start = ((), (), s32[]{:S(2)}) async-start(), calls=%async_computation.43 | async-start | bytes 147456
  1117.3 305.0 %reduce-scatter.42.cloned.1.call-start = ((), (), s32[]{:S(2)}) async-start(), calls=%async_computation.41 | async-start | bytes 737280
  1119.0 332.1 %reduce-scatter.40.cloned.1.call-start = ((), (), s32[]{:S(2)}) async-start(), calls=%async_computation.40 | async-start | bytes 737280
  1124.6 360.0 %reduce-scatter.38.cloned.1.call-start = ((), (), s32[]{:S(2)}) async-start(), calls=%async_computation.39 | async-start | bytes 73728
  1125.2 394.6 %reduce-scatter.34.cloned.1.call-start = ((), (), s32[]{:S(2)}) async-start(), calls=%async_computation.33 | async-start | bytes 2359296 | tf_op jit(solution)/shard_map/reduce_scatter | solution.py:290
  1196.8 427.9 %all-reduce.40.cloned.1.call-start = ((), (), s32[]{:S(2)}) async-start(), calls=%async_computation.44 | async-start | bytes 9175040
  (183 other events, 2554.0 us)
Sparse Core Ops, SparseCore 0:
  11.4 83.2 all-gather.22
  104.3 25.0 all-gather.18
  132.4 63.8 all-gather.24
  199.0 112.4 all-gather.26
  370.6 25.8 all-gather.20
  399.3 70.1 all-gather.28
  732.2 34.9 reduce-scatter.25
  1012.7 34.7 reduce-scatter.27
  1054.2 25.5 reduce-scatter.43
  1083.9 23.3 reduce-scatter.35
  1110.5 86.3 reduce-scatter.31
  1199.8 163.2 reduce-scatter.29
  1365.4 30.5 reduce-scatter.45
  1398.7 23.5 reduce-scatter.41
  1425.6 25.3 reduce-scatter.39
  1453.1 30.5 reduce-scatter.37
  1485.9 33.8 reduce-scatter.33
  1522.0 102.7 all-reduce.39
where the time goes:
time: 1650 us; the launch traced here: 1630 us
  waiting for transfers between devices  661 us (40%)
  local copies, waits for them, and re-layouts  249 us (15%)
  other arithmetic  245 us (15%)
  matrix products  215 us (13%)
  blocking collectives  177 us (11%)
  starting transfers between devices  68 us (4%)
  between operations  18.7 us (1%)
    reduce_scatter x1, waiting for transfers between devices, local(): lax.psum_scatter(stacked[1].astype(jnp.bfloat16), 'batch', scatter_dimens...  166 us
    unnamed x25, waiting for transfers between devices  160 us
    all_gather x2, blocking collectives, local(): lax.all_gather(conv_weight[layer_idx], ('batch', 'seq'), axis=1, tiled=True)  95.1 us
    dot_general x8, matrix products, state_space(): within = jnp.einsum('chts,cshp->cthp', mixing, blocked, precision=HIGHEST)  78.2 us
    unnamed x2, blocking collectives  71.8 us
    reduce_scatter x1, waiting for transfers between devices, local(): lax.psum_scatter(stacked[5].astype(jnp.bfloat16), 'batch', scatter_dimens...  71.6 us
    all_to_all x2, waiting for transfers between devices, local(): lax.all_to_all(d_signal[:, :local_inner].astype(jnp.bfloat16), 'seq', spl...  63.3 us
    unnamed x413, local copies, waits for them, and re-layouts  52 us
  transfers between devices with their start and end apart: 34, of which 20 were waited for; matrix products, arithmetic and copies ran while one was open for 30% of the time, Pallas kernels for 0%

commit v1 on v0

--- a/solution.py
+++ b/solution.py
@@ -9,6 +9,18 @@
 INNER = 2048
 EPS = 1e-05
 HIGHEST = lax.Precision.HIGHEST
+
+
+def doubled_up(x, axis, dim):
+    ways, here = (lax.axis_size(axis), lax.axis_index(axis))
+    grown, reach = (x, 1)
+    while reach < ways:
+        theirs = lax.ppermute(grown, axis, [(d, d ^ reach) for d in range(ways)])
+        mine_first = jnp.concatenate([grown, theirs], axis=dim)
+        theirs_first = jnp.concatenate([theirs, grown], axis=dim)
+        grown = jnp.where(here & reach == 0, mine_first, theirs_first)
+        reach = 2 * reach
+    return grown
 
 
 def row_norm(rows, gain):
@@ -110,7 +122,7 @@
         gathered = (
             lax.all_gather(norm_gain[layer_idx], ("batch", "seq"), axis=0, tiled=True),
             lax.all_gather(in_proj[layer_idx], ("batch", "seq"), axis=0, tiled=True),
-            lax.all_gather(conv_weight[layer_idx], ("batch", "seq"), axis=1, tiled=True),
+            doubled_up(conv_weight[layer_idx], ("batch", "seq"), 1),
             lax.all_gather(conv_bias[layer_idx], ("batch", "seq"), axis=0, tiled=True),
             lax.all_gather(gate_gain[layer_idx], ("batch", "seq"), axis=0, tiled=True),
             lax.all_gather(out_proj[layer_idx], ("batch", "seq"), axis=0, tiled=True),

time: 1650 us -> 1580 us (0.958)
  blocking collectives: 177 us -> 81.5 us
  waiting for transfers between devices: 661 us -> 694 us
    all_gather x2 -> x0, blocking collectives: 95.1 us -> none  [local(): lax.all_gather(conv_weight[layer_idx], ('batch', 'seq'), axis=1, tiled=True)]
    all_gather x2, waiting for transfers between devices: 37.6 us -> 62.7 us  [local(): lax.all_gather(in_proj[layer_idx], ('batch', 'seq'), axis=0, tiled=True)]
    unnamed x413 -> x387, local copies, waits for them, and re-layouts: 52 us -> 49.3 us
  transfers between devices with their start and end apart: 34 -> 44, of which waited for: 20 -> 30; matrix products, arithmetic and copies ran while one was open for 30% -> 30% of each run, Pallas kernels for 0% -> 0%
where the time goes in v1:
time: 1580 us; the launch traced here: 1570 us
  waiting for transfers between devices  694 us (44%)
  other arithmetic  244 us (15%)
  local copies, waits for them, and re-layouts  235 us (15%)
  matrix products  215 us (14%)
  blocking collectives  81.5 us (5%)
  starting transfers between devices  78.4 us (5%)
  between operations  18.7 us (1%)
    reduce_scatter x1, waiting for transfers between devices, local(): lax.psum_scatter(stacked[1].astype(jnp.bfloat16), 'batch', scatter_dimens...  166 us
    unnamed x25, waiting for transfers between devices  159 us
    dot_general x8, matrix products, state_space(): within = jnp.einsum('chts,cshp->cthp', mixing, blocked, precision=HIGHEST)  78.2 us
    reduce_scatter x1, waiting for transfers between devices, local(): lax.psum_scatter(stacked[5].astype(jnp.bfloat16), 'batch', scatter_dimens...  72.2 us
    unnamed x2, blocking collectives  71.6 us
    all_to_all x2, waiting for transfers between devices, local(): lax.all_to_all(d_signal[:, :local_inner].astype(jnp.bfloat16), 'seq', spl...  62.7 us
    all_gather x2, waiting for transfers between devices, local(): lax.all_gather(in_proj[layer_idx], ('batch', 'seq'), axis=0, tiled=True)  62.7 us
    unnamed x387, local copies, waits for them, and re-layouts  49.3 us
  transfers between devices with their start and end apart: 44, of which 30 were waited for; matrix products, arithmetic and copies ran while one was open for 30% of the time, Pallas kernels for 0%

profile of v1, /device:TPU:0, one launch (start us, length us, event | category | flops | bytes accessed | tf_op | source)
XLA Modules:
  0.0 1568.7 jit_solution(2902069534145710987)
XLA Ops:
  12.8 43.3 %all-reduce.36 = (bf16[1024]{0:T(1024)(128)(2,1)S(1)}, bf16[2304]{0:T(1024)(128)(2,1)S(1)}, bf16[2048]{0:T(1024)(128)(2,1)S(1)}, bf16[1024]{0:T(1024)(128)(2,1)S...) all-reduce(bf16[1024]{0:T(1024)(128)(2,1)S(1)} %dynamic-update-slic, ...), channel_id=3, replica_groups=mesh['batch'=4,'seq'=8] {'batch','seq'}, use_global_device_ids=true, to_apply=%add.27 | all-reduce | flops 10752 | bytes 43008
  57.0 37.7 %all-gather.21.cloned.1.call-done = bf16[1,1024,4384]{2,1,0:T(8,128)(2,1)} async-done(((bf16[1,32,4384]{2,1,0:T(8,128)(2,1)}), bf16[1,1024,4384]{2,1,0:T(8,128)(2,1)}) %all-gather.21.cloned.1.call-update) | async-done | bytes 8978448 | tf_op jit(solution)/shard_map/all_gather | solution.py:124
  145.4 26.9 %all-to-all-done = bf16[256,8,256]{0,2,1:T(8,128)(2,1)S(1)} async-done(((bf16[256,8,256]{0,2,1:T(8,128)(2,1)}), bf16[256,8,256]{0,2,1:T(8,128)(2,1)S(1)}, u32[]{:S(2)}, u32[]{:S(2)}) %all-to-all-start) | async-done | bytes 1048608 | tf_op jit(solution)/shard_map/all_to_all | solution.py:138
  229.1 38.7 %all-to-all-done.3 = bf16[8,256,256]{1,2,0:T(8,128)(2,1)S(1)} async-done(((bf16[8,256,256]{1,2,0:T(8,128)(2,1)}), bf16[8,256,256]{1,2,0:T(8,128)(2,1)S(1)}, u32[]{:S(2)}, u32[]{:S(2)}) %all-to-all-start.3) | async-done | bytes 1048608 | tf_op jit(solution)/shard_map/all_to_all | solution.py:168
  276.5 25.0 %all-gather.25.cloned.1.call-done = bf16[1,1024,4384]{2,1,0:T(8,128)(2,1)} async-done(((bf16[1,32,4384]{2,1,0:T(8,128)(2,1)}), bf16[1,1024,4384]{2,1,0:T(8,128)(2,1)}) %all-gather.25.cloned.1.call-update) | async-done | bytes 8978448 | tf_op jit(solution)/shard_map/all_gather | solution.py:124
  339.2 15.2 all-to-all-done.4
  377.7 18.9 %while.95 = (s32[]{:T(128)}, f32[1,4,64,128]{3,2,1,0:T(8,128)S(1)}, f32[8,1,4,64,128]{4,3,2,1,0:T(8,128)}, f32[8,1,4]{2,1,0:T(1,128)}, f32[8,1,4,64,128]{4,3,2,1,0:T(8,128)}, /*index=5*/s32[]{:T(128)}, s32[]{:T(128)}) while((s32[]{:T(128)}, f32[1,4,64,128]{3,2,1,0:T(8,128)S(1)}, f32[8,1,4,64,128]{4,3,2,1,0:T(8,128)}, ...), condition=%wide.region_10.11_spmd.clone, body=%wide.region_9.10_spmd.clone.sunk | while | flops 131075 | bytes 655516 | solution.py:69
  452.4 10.1 all-to-all-done.7
  483.1 22.5 %while.96 = (s32[]{:T(128)}, f32[1,4,64,128]{3,2,1,0:T(8,128)S(1)}, f32[8,1,4,64,128]{4,3,2,1,0:T(8,128)S(1)}, f32[8,1,4,1,1]{2,4,3,1,0:T(1,128)}, f32[8,1,4]{2,...) while((s32[]{:T(128)}, f32[1,4,64,128]{3,2,1,0:T(8,128)S(1)}, ...), condition=%wide.region_15.17_spmd.clone, body=%wide.region_14.16_spmd.clone.sunk | while | flops 131075 | bytes 656552 | solution.py:69
  516.8 13.4 fusion.53
  537.4 19.3 %while.97 = (s32[]{:T(128)}, f32[1,4,64,128]{3,2,1,0:T(8,128)S(1)}, f32[8,1,4,64,128]{4,3,2,1,0:T(8,128)}, f32[8,1,4]{2,1,0:T(1,128)S(1)}, f32[8,1,4,64,128]{4,3...) while((s32[]{:T(128)}, f32[1,4,64,128]{3,2,1,0:T(8,128)S(1)}, ...), condition=%wide.region_19.21_spmd.clone, body=%wide.region_17.20_spmd.clone.sunk | while | flops 196608 | bytes 787668 | solution.py:69
  567.4 10.3 reduce-window.50
  624.8 10.4 bitcast_add_fusion.8
  673.5 30.9 %all-to-all-done.10 = bf16[8,256,256]{1,2,0:T(8,128)(2,1)S(1)} async-done(((bf16[8,256,256]{1,2,0:T(8,128)(2,1)}), bf16[8,256,256]{1,2,0:T(8,128)(2,1)S(1)}, u32[]{:S(2)}, u32[]{:S(2)}) %all-to-all-start.10) | async-done | bytes 1048608 | tf_op jit(solution)/shard_map/all_to_all | solution.py:208
  756.8 23.6 %while.98 = (s32[]{:T(128)}, f32[1,4,64,128]{3,2,1,0:T(8,128)S(1)}, f32[8,1,4,64,128]{4,3,2,1,0:T(8,128)}, f32[8,1,4,1,1]{2,4,3,1,0:T(1,128)S(1)}, f32[8,1,4]{2,...) while((s32[]{:T(128)}, f32[1,4,64,128]{3,2,1,0:T(8,128)S(1)}, ...), condition=%wide.region_34.36_spmd.clone, body=%wide.region_33.35_spmd.clone.sunk | while | flops 131075 | bytes 656056 | solution.py:69
  789.9 13.8 fusion.55
  810.7 19.4 %while.99 = (s32[]{:T(128)}, f32[1,4,64,128]{3,2,1,0:T(8,128)S(1)}, f32[8,1,4,64,128]{4,3,2,1,0:T(8,128)}, f32[8,1,4]{2,1,0:T(1,128)S(1)}, f32[8,1,4,64,128]{4,3...) while((s32[]{:T(128)}, f32[1,4,64,128]{3,2,1,0:T(8,128)S(1)}, ...), condition=%wide.region_38.40_spmd.clone, body=%wide.region_36.39_spmd.clone.sunk | while | flops 196608 | bytes 787668 | solution.py:69
  840.7 10.1 reduce-window.56
  897.0 10.6 bitcast_add_fusion.6
  945.5 31.8 %all-to-all-done.14 = bf16[8,256,256]{1,2,0:T(8,128)(2,1)} async-done(((bf16[8,256,256]{1,2,0:T(8,128)(2,1)}), bf16[8,256,256]{1,2,0:T(8,128)(2,1)}, u32[]{:S(2)}, u32[]{:S(2)}) %all-to-all-start.14) | async-done | bytes 1048608 | tf_op jit(solution)/shard_map/all_to_all | solution.py:208
  992.6 15.5 all-to-all-done.13
  1038.2 11.5 pad_maximum_fusion
  1058.8 72.2 %reduce-scatter.32.cloned.1.call-done = bf16[2,512,1024]{2,1,0:T(8,128)(2,1)} async-done(((bf16[2,2048,1024]{2,1,0:T(8,128)(2,1)}), bf16[2,512,1024]{2,1,0:T(8,128)(2,1)}) %reduce-scatter.32.cloned.1.call-update) | async-done | bytes 2097168 | tf_op jit(solution)/shard_map/reduce_scatter | solution.py:282
  1131.1 166.3 %reduce-scatter.30.cloned.1.call-done = bf16[2,256,4384]{1,2,0:T(8,128)(2,1)} async-done(((bf16[2,1024,4384]{1,2,0:T(8,128)(2,1)}), bf16[2,256,4384]{1,2,0:T(8,128)(2,1)}) %reduce-scatter.30.cloned.1.call-update) | async-done | bytes 4489232 | tf_op jit(solution)/shard_map/reduce_scatter | solution.py:270
  1297.4 12.5 copy.1284
  1317.5 12.8 reduce-scatter.46.cloned.1.call-done
  1331.9 9.9 all-reduce.35
  1343.5 13.1 reduce-scatter.42.cloned.1.call-done
  1357.6 27.8 %reduce-scatter.40.cloned.1.call-done = bf16[576,8]{1,0:T(8,128)(2,1)} async-done(((bf16[2304,8]{1,0:T(8,128)(2,1)}), bf16[576,8]{1,0:T(8,128)(2,1)}) %reduce-scatter.40.cloned.1.call-update) | async-done | bytes 9232
  1386.6 28.3 %all-reduce.37 = (bf16[2,4,576]{2,1,0:T(4,128)(2,1)S(1)}, bf16[2,576]{1,0:T(2,128)(2,1)S(1)}) all-reduce(bf16[2,4,576]{2,1,0:T(4,128)(2,1)S(1)} %copy.1345, bf16[2,576]{1,0:T(2,128)(2,1)S(1)} %copy.1349), channel_id=19, replica_groups=mesh['batch'=4,'seq'=8] {'seq'}, use_global_device_ids=true, to_apply=%region_65.67.clone | all-reduce | flops 5760 | bytes 23040
  1420.4 34.2 %reduce-scatter.34.cloned.1.call-done = bf16[2,64,1024]{2,1,0:T(8,128)(2,1)} async-done(((bf16[2,512,1024]{2,1,0:T(8,128)(2,1)}), bf16[2,64,1024]{2,1,0:T(8,128)(2,1)}) %reduce-scatter.34.cloned.1.call-update) | async-done | bytes 262160 | tf_op jit(solution)/shard_map/reduce_scatter | solution.py:302
  1456.4 102.7 %all-reduce.40.cloned.1.call-done = bf16[2,256,4384]{2,0,1:T(2,128)(2,1)} async-done(((bf16[2,256,4384]{2,0,1:T(2,128)(2,1)}), bf16[2,256,4384]{2,0,1:T(2,128)(2,1)}) %all-reduce.40.cloned.1.call-update) | async-done | bytes 4489232
  (1008 shorter events, 714.9 us)
Async XLA Ops:
  7.2 87.5 %all-gather.21.cloned.1.call-start = ((), (), s32[]{:S(2)}) async-start(), calls=%async_computation.34 | async-start | bytes 9461760 | tf_op jit(solution)/shard_map/all_gather | solution.py:124
  9.2 168.7 %all-gather.17.cloned.1.call-start = ((), (), s32[]{:S(2)}) async-start(), calls=%async_computation.27 | async-start | bytes 1179648 | tf_op jit(solution)/shard_map/all_gather | solution.py:142
  104.2 168.0 %all-gather.23.cloned.1.call-start = ((), (), s32[]{:S(2)}) async-start(), calls=%async_computation.35 | async-start | bytes 4325376 | tf_op jit(solution)/shard_map/all_gather | solution.py:128
  105.0 196.5 %all-gather.25.cloned.1.call-start = ((), (), s32[]{:S(2)}) async-start(), calls=%async_computation.36 | async-start | bytes 9461760 | tf_op jit(solution)/shard_map/all_gather | solution.py:124
  134.4 37.9 %all-to-all-start = ((bf16[256,8,256]{0,2,1:T(8,128)(2,1)}), bf16[256,8,256]{0,2,1:T(8,128)(2,1)S(1)}, u32[]{:S(2)}, u32[]{:S(2)}) async-start(bf16[256,8,256]{0,2,1:T(8,128)(2,1)} %bitcast.5), calls=%async_computation | async-start | bytes 2097152 | tf_op jit(solution)/shard_map/all_to_all | solution.py:138
  172.3 41.1 %all-to-all-start.2 = ((bf16[256,8,256]{0,2,1:T(8,128)(2,1)}), bf16[256,8,256]{0,2,1:T(8,128)(2,1)}, u32[]{:S(2)}, u32[]{:S(2)}) async-start(bf16[256,8,256]{0,2,1:T(8,128)(2,1)} %bitcast.38), calls=%async_computation.2 | async-start | bytes 2097152 | tf_op jit(solution)/shard_map/all_to_all | solution.py:139
  225.4 42.3 %all-to-all-start.3 = ((bf16[8,256,256]{1,2,0:T(8,128)(2,1)}), bf16[8,256,256]{1,2,0:T(8,128)(2,1)S(1)}, u32[]{:S(2)}, u32[]{:S(2)}) async-start(bf16[8,256,256]{1,2,0:T(8,128)(2,1)} %copy.1153), calls=%async_computation.3 | async-start | bytes 2097152 | tf_op jit(solution)/shard_map/all_to_all | solution.py:168
  229.0 130.9 %all-gather.19.cloned.1.call-start = ((), (), s32[]{:S(2)}) async-start(), calls=%async_computation.28 | async-start | bytes 1179648 | tf_op jit(solution)/shard_map/all_gather | solution.py:142
  310.9 158.6 %all-gather.27.cloned.1.call-start = ((), (), s32[]{:S(2)}) async-start(), calls=%async_computation.37 | async-start | bytes 4325376 | tf_op jit(solution)/shard_map/all_gather | solution.py:128
  322.6 31.9 %all-to-all-start.4 = ((bf16[256,8,256]{0,2,1:T(8,128)(2,1)}), bf16[256,8,256]{0,2,1:T(8,128)(2,1)S(1)}, u32[]{:S(2)}, u32[]{:S(2)}) async-start(bf16[256,8,256]{0,2,1:T(8,128)(2,1)} %bitcast.49), calls=%async_computation.4 | async-start | bytes 2097152 | tf_op jit(solution)/shard_map/all_to_all | solution.py:138
  354.5 63.4 %all-to-all-start.6 = ((bf16[256,8,256]{0,2,1:T(8,128)(2,1)}), bf16[256,8,256]{0,2,1:T(8,128)(2,1)}, u32[]{:S(2)}, u32[]{:S(2)}) async-start(bf16[256,8,256]{0,2,1:T(8,128)(2,1)} %bitcast.82), calls=%async_computation.6 | async-start | bytes 2097152 | tf_op jit(solution)/shard_map/all_to_all | solution.py:139
  430.8 31.6 %all-to-all-start.7 = ((bf16[8,256,256]{1,2,0:T(8,128)(2,1)}), bf16[8,256,256]{1,2,0:T(8,128)(2,1)}, u32[]{:S(2)}, u32[]{:S(2)}) async-start(bf16[8,256,256]{1,2,0:T(8,128)(2,1)} %copy.1178), calls=%async_computation.7 | async-start | bytes 2097152 | tf_op jit(solution)/shard_map/all_to_all | solution.py:168
  478.0 31.0 %all-to-all-start.8 = ((bf16[256,8,256]{0,2,1:T(8,128)(2,1)}), bf16[256,8,256]{0,2,1:T(8,128)(2,1)}, u32[]{:S(2)}, u32[]{:S(2)}) async-start(bf16[256,8,256]{0,2,1:T(8,128)(2,1)} %bitcast.113), calls=%async_computation.8 | async-start | bytes 2097152 | tf_op jit(solution)/shard_map/all_to_all | solution.py:195
  592.0 73.9 %all-to-all-start.11 = ((bf16[8,256,4]{1,2,0:T(4,128)(2,1)}), bf16[8,256,4]{1,2,0:T(4,128)(2,1)S(1)}, u32[]{:S(2)}, u32[]{:S(2)}) async-start(bf16[8,256,4]{1,2,0:T(4,128)(2,1)} %bitcast.161), calls=%async_computation.12 | async-start | bytes 32768 | tf_op jit(solution)/shard_map/all_to_all | solution.py:222
  666.0 38.5 %all-to-all-start.10 = ((bf16[8,256,256]{1,2,0:T(8,128)(2,1)}), bf16[8,256,256]{1,2,0:T(8,128)(2,1)S(1)}, u32[]{:S(2)}, u32[]{:S(2)}) async-start(bf16[8,256,256]{1,2,0:T(8,128)(2,1)} %bitcast.912), calls=%async_computation.10 | async-start | bytes 2097152 | tf_op jit(solution)/shard_map/all_to_all | solution.py:208
  671.2 64.0 %reduce-scatter.26.cloned.1.call-start = ((), (), s32[]{:S(2)}) async-start(), calls=%async_computation.29 | async-start | bytes 1179648 | tf_op jit(solution)/shard_map/reduce_scatter | solution.py:230
  704.5 30.8 %all-to-all-start.9 = ((bf16[8,256,256]{1,2,0:T(8,128)(2,1)}), bf16[8,256,256]{1,2,0:T(8,128)(2,1)}, u32[]{:S(2)}, u32[]{:S(2)}) async-start(bf16[8,256,256]{1,2,0:T(8,128)(2,1)} %copy.1203), calls=%async_computation.9 | async-start | bytes 2097152 | tf_op jit(solution)/shard_map/all_to_all | solution.py:215
  751.0 31.3 %all-to-all-start.12 = ((bf16[256,8,256]{0,2,1:T(8,128)(2,1)}), bf16[256,8,256]{0,2,1:T(8,128)(2,1)}, u32[]{:S(2)}, u32[]{:S(2)}) async-start(bf16[256,8,256]{0,2,1:T(8,128)(2,1)} %bitcast.990), calls=%async_computation.13 | async-start | bytes 2097152 | tf_op jit(solution)/shard_map/all_to_all | solution.py:195
  864.1 73.8 %all-to-all-start.15 = ((bf16[8,256,4]{1,2,0:T(4,128)(2,1)}), bf16[8,256,4]{1,2,0:T(4,128)(2,1)S(1)}, u32[]{:S(2)}, u32[]{:S(2)}) async-start(bf16[8,256,4]{1,2,0:T(4,128)(2,1)} %bitcast.236), calls=%async_computation.17 | async-start | bytes 32768 | tf_op jit(solution)/shard_map/all_to_all | solution.py:222
  937.9 39.4 %all-to-all-start.14 = ((bf16[8,256,256]{1,2,0:T(8,128)(2,1)}), bf16[8,256,256]{1,2,0:T(8,128)(2,1)}, u32[]{:S(2)}, u32[]{:S(2)}) async-start(bf16[8,256,256]{1,2,0:T(8,128)(2,1)} %bitcast.911), calls=%async_computation.15 | async-start | bytes 2097152 | tf_op jit(solution)/shard_map/all_to_all | solution.py:208
  943.2 64.9 %reduce-scatter.28.cloned.1.call-start = ((), (), s32[]{:S(2)}) async-start(), calls=%async_computation.30 | async-start | bytes 1179648 | tf_op jit(solution)/shard_map/reduce_scatter | solution.py:230
  977.3 30.8 %all-to-all-start.13 = ((bf16[8,256,256]{1,2,0:T(8,128)(2,1)}), bf16[8,256,256]{1,2,0:T(8,128)(2,1)}, u32[]{:S(2)}, u32[]{:S(2)}) async-start(bf16[8,256,256]{1,2,0:T(8,128)(2,1)} %copy.1255), calls=%async_computation.14 | async-start | bytes 2097152 | tf_op jit(solution)/shard_map/all_to_all | solution.py:215
  981.6 69.3 %reduce-scatter.44.cloned.1.call-start = ((), (), s32[]{:S(2)}) async-start(), calls=%async_computation.42 | async-start | bytes 655360
  987.6 70.6 %reduce-scatter.36.cloned.1.call-start = ((), (), s32[]{:S(2)}) async-start(), calls=%async_computation.38 | async-start | bytes 327680
  1017.4 113.7 %reduce-scatter.32.cloned.1.call-start = ((), (), s32[]{:S(2)}) async-start(), calls=%async_computation.32 | async-start | bytes 10485760 | tf_op jit(solution)/shard_map/reduce_scatter | solution.py:282
  1025.0 272.4 %reduce-scatter.30.cloned.1.call-start = ((), (), s32[]{:S(2)}) async-start(), calls=%async_computation.31 | async-start | bytes 22446080 | tf_op jit(solution)/shard_map/reduce_scatter | solution.py:270
  1049.8 280.5 %reduce-scatter.46.cloned.1.call-start = ((), (), s32[]{:S(2)}) async-start(), calls=%async_computation.43 | async-start | bytes 147456
  1050.9 305.8 %reduce-scatter.42.cloned.1.call-start = ((), (), s32[]{:S(2)}) async-start(), calls=%async_computation.41 | async-start | bytes 737280
  1052.5 332.9 %reduce-scatter.40.cloned.1.call-start = ((), (), s32[]{:S(2)}) async-start(), calls=%async_computation.40 | async-start | bytes 737280
  1058.2 360.8 %reduce-scatter.38.cloned.1.call-start = ((), (), s32[]{:S(2)}) async-start(), calls=%async_computation.39 | async-start | bytes 73728
  1058.8 395.8 %reduce-scatter.34.cloned.1.call-start = ((), (), s32[]{:S(2)}) async-start(), calls=%async_computation.33 | async-start | bytes 2359296 | tf_op jit(solution)/shard_map/reduce_scatter | solution.py:302
  1131.1 428.0 %all-reduce.40.cloned.1.call-start = ((), (), s32[]{:S(2)}) async-start(), calls=%async_computation.44 | async-start | bytes 9175040
  (180 other events, 2826.4 us)
Sparse Core Ops, SparseCore 0:
  11.4 83.2 all-gather.20
  104.3 22.6 all-gather.16
  129.9 71.8 all-gather.22
  204.5 96.8 all-gather.24
  311.0 25.3 all-gather.18
  339.3 69.7 all-gather.26
  674.9 35.1 reduce-scatter.25
  946.3 35.0 reduce-scatter.27
  987.7 26.3 reduce-scatter.43
  1017.5 24.0 reduce-scatter.35
  1044.7 86.2 reduce-scatter.31
  1134.1 163.2 reduce-scatter.29
  1299.6 30.5 reduce-scatter.45
  1333.0 23.6 reduce-scatter.41
  1359.9 25.4 reduce-scatter.39
  1387.5 30.5 reduce-scatter.37
  1420.2 34.3 reduce-scatter.33
  1456.8 102.2 all-reduce.39
